TPU v7x, 256 devices: a whole 4x4x8 slice. The times are simulated.
256 devices in a mesh: dp: 32 (over x, y, core), type: 8 (over z).
Axes of the slice: x: 4, y: 4, z: 8, core: 2. Of those that a mesh axis runs over, the one named last changes fastest.
Arguments:
- tokens: bfloat16 [32768, 4096], P(('dp', 'type')), may hold values from -6 to 6
- token_types: int32 [32768, 1], P(('dp', 'type')), may hold values from 0 to 7
- tile_mask: int32 [32, 8, 8], P('dp', 'type'), may hold values from 0 to 1, as said below
- queries: bfloat16 [32768, 4096], P(('dp', 'type')), may hold values from -60 to 60
- keys: bfloat16 [32768, 4096], P(('dp', 'type')), may hold values from -4 to 4
- gate_weight: bfloat16 [8, 4096, 7168], P('type', None, 'dp'), may hold values from -0.09375 to 0.09375
- up_weight: bfloat16 [8, 4096, 7168], P('type', None, 'dp'), may hold values from -0.09375 to 0.09375
- down_weight: bfloat16 [8, 7168, 4096], P('type', 'dp'), may hold values from -0.0625 to 0.0625
Outputs:
- expert_out: bfloat16 [32768, 4096], P(('dp', 'type'))
- attended: bfloat16 [32768, 4096], P(('dp', 'type'))
Inputs may be any that keep to these rules, and one draw needn't show every extreme that they name: `tile_mask`: every diagonal entry is 1.
All inputs are finite; a program needn't handle non-finite values.
Results may differ from a plain program's by a relative error of at most 0.02.
Values may be sent and summed in bfloat16 or wider, within the bound.
A program may use at most 128 MiB of HBM per device.

v0:
```python
import math
import jax
import jax.numpy as jnp
from jax import lax
from jax.sharding import PartitionSpec as P

HEAD = 128
EXP_CAP = 16


def on_device(tokens, token_types, tile_mask, queries, keys, gate_weight, up_weight, down_weight):
    n_type = lax.axis_size("type")
    my_index = lax.axis_index("type")
    tok_rows = tokens.shape[0]
    feat_width = tokens.shape[1]
    type_ids = jnp.arange(n_type, dtype=jnp.int32)
    slot_ids = jnp.arange(EXP_CAP, dtype=jnp.int32)
    keys_all = lax.all_gather(keys, "type", axis=0, tiled=True)
    event_types = lax.all_gather(token_types[:, 0], "type", axis=0, tiled=True)
    hot = (event_types[None, :] == type_ids[:, None]).astype(jnp.int32)
    rank = jnp.cumsum(hot, axis=1) - hot
    place = (
        ((rank[:, None, :] == slot_ids[None, :, None]) & (hot[:, None, :] == 1))
        .astype(jnp.bfloat16)
        .reshape(n_type * EXP_CAP, n_type * tok_rows)
    )
    own_place = lax.dynamic_slice_in_dim(place, my_index * tok_rows, tok_rows, 1)
    contrib = jnp.dot(own_place, tokens, preferred_element_type=jnp.float32).astype(jnp.bfloat16)
    packed = lax.psum_scatter(contrib, "type", scatter_dimension=0, tiled=True)
    block_rows = lax.all_gather(packed, "dp", axis=0, tiled=True)
    gate_act = jnp.dot(block_rows, gate_weight[0], preferred_element_type=jnp.float32)
    up_act = jnp.dot(block_rows, up_weight[0], preferred_element_type=jnp.float32)
    hidden = (jax.nn.silu(gate_act) * up_act).astype(jnp.bfloat16)
    partial_terms = jnp.dot(hidden, down_weight[0], preferred_element_type=jnp.float32)
    summed = lax.psum_scatter(
        partial_terms.astype(jnp.bfloat16), "dp", scatter_dimension=0, tiled=True
    )
    slot_values = lax.all_gather(summed, "type", axis=0, tiled=True)
    expert_out = jnp.einsum(
        "pt,pd->td", own_place, slot_values, preferred_element_type=jnp.float32
    ).astype(jnp.bfloat16)
    mask_row = tile_mask[0, 0]
    allowed = jnp.repeat(mask_row == 1, tok_rows)
    head_count = feat_width // HEAD
    query_heads = queries.reshape(tok_rows, head_count, HEAD)
    key_heads = keys_all.reshape(-1, head_count, HEAD)
    value_heads = slot_values.reshape(-1, head_count, HEAD)
    scores = jnp.einsum(
        "qhd,khd->hqk", query_heads, key_heads, preferred_element_type=jnp.float32
    ) * (1.0 / math.sqrt(HEAD))
    masked = jnp.where(allowed[None, None, :], scores, -jnp.inf)
    row_max = jnp.max(masked, axis=-1, keepdims=True)
    weights = jnp.where(allowed[None, None, :], jnp.exp(masked - row_max), 0.0).astype(jnp.bfloat16)
    total_weight = jnp.sum(weights.astype(jnp.float32), axis=-1)
    slot_weights = jnp.einsum(
        "hqk,pk->hqp", weights, place, preferred_element_type=jnp.float32
    ).astype(jnp.bfloat16)
    attended = (
        jnp.einsum("hqp,phd->qhd", slot_weights, value_heads, preferred_element_type=jnp.float32)
        / jnp.transpose(total_weight)[:, :, None]
    )
    return (expert_out, attended.reshape(tok_rows, feat_width).astype(jnp.bfloat16))


def solution(mesh):
    return jax.shard_map(
        on_device,
        mesh=mesh,
        in_specs=(
            P(("dp", "type"), None),
            P(("dp", "type"), None),
            P("dp", "type", None),
            P(("dp", "type"), None),
            P(("dp", "type"), None),
            P("type", None, "dp"),
            P("type", None, "dp"),
            P("type", "dp", None),
        ),
        out_specs=(P(("dp", "type"), None), P(("dp", "type"), None)),
        check_vma=False,
    )
```

profile of v0, /device:TPU:2, one launch (start us, length us, event | category | flops | bytes accessed | tf_op | source)
XLA Modules:
  0.0 382.4 jit_solution(15770409194891240785)
XLA Ops:
  7.2 0.0 copy-start
  7.2 0.0 reduce-scatter.3.cloned.1.call-start
  7.2 19.4 %all-gather = s32[1024,1]{0,1:T(1,128)S(1)} all-gather(s32[128,1]{0,1:T(1,128)} %param.9), channel_id=2, replica_groups=mesh['dp'=32,'type'=8] {'type'}, dimensions={0}, use_global_device_ids=true | all-gather | bytes 4608 | tf_op jit(solution)/shard_map/all_gather | solution.py:19
  26.7 0.1 eq.76
  26.8 2.3 reduce-window.6
  29.1 0.3 slice_reduce_fusion
  29.3 0.2 reduce-window.9
  29.5 0.1 add_bitcast_fusion
  29.6 0.2 fusion.22
  29.8 2.6 convolution_convert_fusion.2
  32.4 0.0 reduce-scatter.3.cloned.1.call-update
  32.4 0.0 all-gather.5.cloned.1.call-start
  32.5 37.2 %reduce-scatter.3.cloned.1.call-done = bf16[16,4096]{1,0:T(8,128)(2,1)} async-done(((bf16[128,4096]{1,0:T(8,128)(2,1)}), bf16[16,4096]{1,0:T(8,128)(2,1)}) %reduce-scatter.3.cloned.1.call-update) | async-done | bytes 131088 | tf_op jit(solution)/shard_map/reduce_scatter | solution.py:29
  69.7 0.0 all-gather.5.cloned.1.call-update
  69.7 0.0 reduce-scatter.5.cloned.1.call-start
  69.8 51.9 %all-gather.5.cloned.1.call-done = bf16[512,4096]{1,0:T(8,128)(2,1)} async-done(((bf16[16,4096]{1,0:T(8,128)(2,1)}), bf16[512,4096]{1,0:T(8,128)(2,1)}) %all-gather.5.cloned.1.call-update) | async-done | bytes 4194320 | tf_op jit(solution)/shard_map/all_gather | solution.py:30
  121.7 4.2 %fusion.9 = f32[512,224]{0,1:T(8,128)S(1)} fusion(bf16[512,4096]{1,0:T(8,128)(2,1)} %all-gather.5.cloned.1.call-done, bf16[1,4096,224]{1,2,0:T(8,128)(2,1)} %param.13), kind=kOutput, calls=%fused_computation.16 | convolution fusion | flops 939524096 | bytes 6488064 | tf_op jit(solution)/shard_map/dot_general | solution.py:31
  125.9 0.0 copy-done
  125.9 7.4 %convolution_convert_fusion = bf16[512,4096]{1,0:T(8,128)(2,1)} fusion(bf16[1,224,4096]{2,1,0:T(8,128)(2,1)S(1)} %copy-done, bf16[512,4096]{1,0:T(8,128)(2,1)} %all-gather.5.cloned.1.call-done, bf16[1,4096,224]{1,2,0:T(8,128)(2,1)} %param.14, f32[512,224]{0,1:T(8,128)S(1)} %fusion.9), kind=kOutput, calls=%fused_computation.8 | convolution fusion | flops 1881833472 | bytes 12517376 | tf_op jit(solution)/shard_map/dot_general | solution.py:34
  133.3 0.0 copy-start.3
  133.3 0.0 copy-start.2
  133.3 0.0 reduce-scatter.5.cloned.1.call-update
  133.3 0.0 all-gather.9.cloned.1.call-start
  133.4 2.3 copy.13
  135.7 0.0 all-gather.9.cloned.1.call-update
  135.7 0.2 all-gather.7.cloned.1.call-start
  136.0 0.0 copy-done.3
  136.0 0.1 broadcast_bitcast_fusion
  136.1 86.8 %reduce-scatter.5.cloned.1.call-done = bf16[16,4096]{1,0:T(8,128)(2,1)} async-done(((bf16[512,4096]{1,0:T(8,128)(2,1)}), bf16[16,4096]{1,0:T(8,128)(2,1)}) %reduce-scatter.5.cloned.1.call-update) | async-done | bytes 131088 | tf_op jit(solution)/shard_map/reduce_scatter | solution.py:35
  222.9 0.0 all-gather.7.cloned.1.call-update
  222.9 100.8 %all-gather.9.cloned.1.call-done = bf16[1024,4096]{0,1:T(8,128)(2,1)} async-done(((bf16[128,4096]{0,1:T(8,128)(2,1)}), bf16[1024,4096]{0,1:T(8,128)(2,1)}) %all-gather.9.cloned.1.call-update) | async-done | bytes 8388624 | tf_op jit(solution)/shard_map/all_gather | solution.py:18
  323.7 0.0 copy-done.2
  323.7 11.4 %fusion.19 = f32[32,128,1024]{2,1,0:T(8,128)} fusion(bf16[1024,32,128]{0,2,1:T(8,128)(2,1)} %bitcast.58, bf16[128,4096]{1,0:T(8,128)(2,1)S(1)} %copy-done.2), kind=kOutput, calls=%fused_computation.21 | convolution fusion | flops 1073741824 | bytes 26214400 | tf_op jit(solution)/shard_map/qhd,khd->hqk/dot_general | solution.py:48
  335.1 18.0 %convert_reduce_fusion = (f32[32,128]{1,0:T(8,128)S(1)}, bf16[32,128,1024]{2,1,0:T(8,128)(2,1)}) fusion(f32[32,128,1024]{2,1,0:T(8,128)} %fusion.19, pred[1024]{0:T(1024)(128)(4,1)S(1)} %broadcast_bitcast_fusion), kind=kOutput, calls=%fused_computation.1 | output fusion | flops 37749760 | bytes 25183232 | tf_op jit(solution)/shard_map/sub | solution.py:53
  353.1 8.8 %all-gather.7.cloned.1.call-done = bf16[128,4096]{1,0:T(8,128)(2,1)} async-done(((bf16[16,4096]{1,0:T(8,128)(2,1)}), bf16[128,4096]{1,0:T(8,128)(2,1)}) %all-gather.7.cloned.1.call-update) | async-done | bytes 1048592 | tf_op jit(solution)/shard_map/all_gather | solution.py:38
  361.9 2.3 copy.19
  364.2 0.0 copy-start.1
  364.2 8.0 %fusion.5 = bf16[128,32,128]{0,2,1:T(8,128)(2,1)} fusion(bf16[128,32,128]{0,2,1:T(8,128)(2,1)} %bitcast.59, bf16[32,128,1024]{2,1,0:T(8,128)(2,1)} %get-tuple-element.7, f32[128,32]{0,1:T(8,128)S(1)} %bitcast.65, pred[128,1024]{1,0:T(32,128)(4,1)S(1)} %fusion.22), kind=kOutput, calls=%fused_computation.12 | convolution fusion | flops 1209532416 | bytes 10633216 | tf_op jit(solution)/shard_map/hqp,phd->qhd/dot_general | solution.py:59
  372.2 2.3 copy.17
  374.4 0.0 copy-done.1
  374.4 1.5 convolution_convert_fusion.1
  (5 shorter events, 0.0 us)
Async XLA Ops:
  7.2 118.7 %copy-start = (bf16[1,224,4096]{2,1,0:T(8,128)(2,1)S(1)}, bf16[1,224,4096]{2,1,0:T(8,128)(2,1)}, u32[]{:S(2)}) copy-start(bf16[1,224,4096]{2,1,0:T(8,128)(2,1)} %param.15) | copy-start | bytes 5505028
  7.2 62.5 %reduce-scatter.3.cloned.1.call-start = ((), (), s32[]{:S(2)}) async-start(), calls=%async_computation.2 | async-start | bytes 1179648 | tf_op jit(solution)/shard_map/reduce_scatter | solution.py:29
  32.4 89.2 %all-gather.5.cloned.1.call-start = ((), (), s32[]{:S(2)}) async-start(), calls=%async_computation.3 | async-start | bytes 4325376 | tf_op jit(solution)/shard_map/all_gather | solution.py:30
  69.7 153.1 %reduce-scatter.5.cloned.1.call-start = ((), (), s32[]{:S(2)}) async-start(), calls=%async_computation.4 | async-start | bytes 4325376 | tf_op jit(solution)/shard_map/reduce_scatter | solution.py:35
  133.3 2.7 copy-start.3
  133.3 190.4 %copy-start.2 = (bf16[128,4096]{1,0:T(8,128)(2,1)S(1)}, bf16[128,4096]{1,0:T(8,128)(2,1)}, u32[]{:S(2)}) copy-start(bf16[128,4096]{1,0:T(8,128)(2,1)} %param.11) | copy-start | bytes 3145732
  133.3 190.4 %all-gather.9.cloned.1.call-start = ((), (), s32[]{:S(2)}) async-start(), calls=%async_computation.6 | async-start | bytes 9437184 | tf_op jit(solution)/shard_map/all_gather | solution.py:18
  135.7 226.2 %all-gather.7.cloned.1.call-start = ((), (), s32[]{:S(2)}) async-start(), calls=%async_computation.5 | async-start | bytes 1179648 | tf_op jit(solution)/shard_map/all_gather | solution.py:38
  364.2 10.2 %copy-start.1 = (bf16[128,4096]{1,0:T(8,128)(2,1)S(1)}, bf16[128,4096]{1,0:T(8,128)(2,1)}, u32[]{:S(2)}) copy-start(bf16[128,4096]{1,0:T(8,128)(2,1)} %all-gather.7.cloned.1.call-done) | copy-start | bytes 3145732
Sparse Core Ops, SparseCore 0:
  32.6 37.1 reduce-scatter.2
  72.3 49.3 all-gather.4
  133.4 89.3 reduce-scatter.4
  225.0 98.6 all-gather.8
  325.3 36.5 all-gather.6
where the time goes:
time: 383 us; the launch traced here: 382 us
  waiting for transfers between devices  286 us (75%)
  matrix products  35.1 us (9%)
  other arithmetic  20.7 us (5%)
  blocking collectives  19.4 us (5%)
  between operations  13.9 us (4%)
  local copies, waits for them, and re-layouts  7.32 us (2%)
    all_gather x1, waiting for transfers between devices, on_device(): keys_all = lax.all_gather(keys, 'type', axis=0, tiled=True)  101 us
    reduce_scatter x1, waiting for transfers between devices, on_device(): lax.psum_scatter(partial_terms.astype(jnp.bfloat16), 'dp', scatter_dimens...  86.8 us
    all_gather x1, waiting for transfers between devices, on_device(): block_rows = lax.all_gather(packed, 'dp', axis=0, tiled=True)  51.9 us
    reduce_scatter x1, waiting for transfers between devices, on_device(): packed = lax.psum_scatter(contrib, 'type', scatter_dimension=0, tiled=True)  37.2 us
    all_gather x1, blocking collectives, on_device(): event_types = lax.all_gather(token_types[:, 0], 'type', axis=0, tiled=True)  19.4 us
    sub x1, other arithmetic, on_device(): masked - row_max  18 us
    dot_general x1, matrix products, on_device(): jnp.einsum('qhd,khd->hqk', query_heads, key_heads, preferred_element_type...  11.4 us
    all_gather x1, waiting for transfers between devices, on_device(): slot_values = lax.all_gather(summed, 'type', axis=0, tiled=True)  8.81 us
  transfers between devices with their start and end apart: 5, of which 5 were waited for; matrix products, arithmetic and copies ran while one was open for 8% of the time, Pallas kernels for 0%

commit v1 on v0

--- a/solution.py
+++ b/solution.py
@@ -35,7 +35,15 @@
     summed = lax.psum_scatter(
         partial_terms.astype(jnp.bfloat16), "dp", scatter_dimension=0, tiled=True
     )
-    slot_values = lax.all_gather(summed, "type", axis=0, tiled=True)
+    slot_values = jnp.concatenate(
+        lax.all_to_all(
+            jnp.stack(lax.axis_size("type") * [summed]),
+            axis_name="type",
+            split_axis=0,
+            concat_axis=0,
+        ),
+        axis=0,
+    )
     expert_out = jnp.einsum(
         "pt,pd->td", own_place, slot_values, preferred_element_type=jnp.float32
     ).astype(jnp.bfloat16)

time: 383 us -> 389 us (1.016)
  starting transfers between devices: 0.38 us -> 7.19 us
    all_gather x1, waiting for transfers between devices: 101 us -> 110 us  [on_device(): keys_all = lax.all_gather(keys, 'type', axis=0, tiled=True)]
    all_gather x1 -> x0, waiting for transfers between devices: 8.81 us -> none  [on_device(): slot_values = lax.all_gather(summed, 'type', axis=0, tiled=True)]
    all_to_all x0 -> x1, starting transfers between devices: none -> 7.03 us  [on_device(): lax.all_to_all(jnp.stack(lax.axis_size('type') * [summed]), axis_name='ty...]
  transfers between devices with their start and end apart: 5 -> 5, of which waited for: 5 -> 4; matrix products, arithmetic and copies ran while one was open for 8% -> 9% of each run, Pallas kernels for 0% -> 0%
where the time goes in v1:
time: 389 us
  waiting for transfers between devices  286 us (74%)
  matrix products  34.4 us (9%)
  other arithmetic  20.7 us (5%)
  blocking collectives  19.4 us (5%)
  between operations  13.9 us (4%)
  local copies, waits for them, and re-layouts  7.38 us (2%)
  starting transfers between devices  7.19 us (2%)
    all_gather x1, waiting for transfers between devices, on_device(): keys_all = lax.all_gather(keys, 'type', axis=0, tiled=True)  110 us
    reduce_scatter x1, waiting for transfers between devices, on_device(): lax.psum_scatter(partial_terms.astype(jnp.bfloat16), 'dp', scatter_dimens...  86.9 us
    all_gather x1, waiting for transfers between devices, on_device(): block_rows = lax.all_gather(packed, 'dp', axis=0, tiled=True)  51.9 us
    reduce_scatter x1, waiting for transfers between devices, on_device(): packed = lax.psum_scatter(contrib, 'type', scatter_dimension=0, tiled=True)  37.2 us
    all_gather x1, blocking collectives, on_device(): event_types = lax.all_gather(token_types[:, 0], 'type', axis=0, tiled=True)  19.4 us
    sub x1, other arithmetic, on_device(): masked - row_max  18 us
    dot_general x1, matrix products, on_device(): jnp.einsum('qhd,khd->hqk', query_heads, key_heads, preferred_element_type...  11.8 us
  transfers between devices with their start and end apart: 5, of which 4 were waited for; matrix products, arithmetic and copies ran while one was open for 9% of the time, Pallas kernels for 0%

profile of v1, /device:TPU:2, one launch (start us, length us, event | category | flops | bytes accessed | tf_op | source)
XLA Modules:
  0.0 389.0 jit_solution(8195526194786602625)
XLA Ops:
  7.2 0.0 copy-start
  7.2 0.0 reduce-scatter.3.cloned.1.call-start
  7.2 19.4 %all-gather = s32[1024,1]{0,1:T(1,128)S(1)} all-gather(s32[128,1]{0,1:T(1,128)} %param.9), channel_id=2, replica_groups=mesh['dp'=32,'type'=8] {'type'}, dimensions={0}, use_global_device_ids=true | all-gather | bytes 4608 | tf_op jit(solution)/shard_map/all_gather | solution.py:19
  26.7 0.1 eq.76
  26.8 2.3 reduce-window.6
  29.1 0.3 slice_reduce_fusion
  29.3 0.2 reduce-window.9
  29.5 0.1 add_bitcast_fusion
  29.6 0.2 fusion.23
  29.8 2.6 convolution_convert_fusion.2
  32.4 0.0 reduce-scatter.3.cloned.1.call-update
  32.4 0.0 all-gather.4.cloned.1.call-start
  32.5 37.2 %reduce-scatter.3.cloned.1.call-done = bf16[16,4096]{1,0:T(8,128)(2,1)} async-done(((bf16[128,4096]{1,0:T(8,128)(2,1)}), bf16[16,4096]{1,0:T(8,128)(2,1)}) %reduce-scatter.3.cloned.1.call-update) | async-done | bytes 131088 | tf_op jit(solution)/shard_map/reduce_scatter | solution.py:29
  69.7 0.0 all-gather.4.cloned.1.call-update
  69.7 0.0 reduce-scatter.5.cloned.1.call-start
  69.8 51.9 %all-gather.4.cloned.1.call-done = bf16[512,4096]{1,0:T(8,128)(2,1)} async-done(((bf16[16,4096]{1,0:T(8,128)(2,1)}), bf16[512,4096]{1,0:T(8,128)(2,1)}) %all-gather.4.cloned.1.call-update) | async-done | bytes 4194320 | tf_op jit(solution)/shard_map/all_gather | solution.py:30
  121.7 4.2 %fusion.9 = f32[512,224]{0,1:T(8,128)S(1)} fusion(bf16[512,4096]{1,0:T(8,128)(2,1)} %all-gather.4.cloned.1.call-done, bf16[1,4096,224]{1,2,0:T(8,128)(2,1)} %param.13), kind=kOutput, calls=%fused_computation.16 | convolution fusion | flops 939524096 | bytes 6488064 | tf_op jit(solution)/shard_map/dot_general | solution.py:31
  125.9 0.0 copy-done
  125.9 7.4 %convolution_convert_fusion = bf16[512,4096]{1,0:T(8,128)(2,1)} fusion(bf16[1,224,4096]{2,1,0:T(8,128)(2,1)S(1)} %copy-done, bf16[512,4096]{1,0:T(8,128)(2,1)} %all-gather.4.cloned.1.call-done, bf16[1,4096,224]{1,2,0:T(8,128)(2,1)} %param.14, f32[512,224]{0,1:T(8,128)S(1)} %fusion.9), kind=kOutput, calls=%fused_computation.8 | convolution fusion | flops 1881833472 | bytes 12517376 | tf_op jit(solution)/shard_map/dot_general | solution.py:34
  133.3 0.0 copy-start.1
  133.3 0.0 copy-start.2
  133.3 0.0 reduce-scatter.5.cloned.1.call-update
  133.3 0.0 all-gather.6.cloned.1.call-start
  133.4 1.1 copy-done.1
  134.5 1.3 copy.13
  135.8 0.0 all-gather.6.cloned.1.call-update
  135.8 0.0 copy-done.2
  135.9 0.1 broadcast_bitcast_fusion
  135.9 86.9 %reduce-scatter.5.cloned.1.call-done = bf16[16,4096]{1,0:T(8,128)(2,1)} async-done(((bf16[512,4096]{1,0:T(8,128)(2,1)}), bf16[16,4096]{1,0:T(8,128)(2,1)}) %reduce-scatter.5.cloned.1.call-update) | async-done | bytes 131088 | tf_op jit(solution)/shard_map/reduce_scatter | solution.py:35
  222.9 2.0 stack.2
  224.8 7.0 %all-to-all-start = ((bf16[8,16,4096]{2,1,0:T(8,128)(2,1)}), bf16[8,16,4096]{2,1,0:T(8,128)(2,1)S(1)}, u32[]{:S(2)}, u32[]{:S(2)}) async-start(bf16[8,16,4096]{2,1,0:T(8,128)(2,1)} %stack.2), calls=%async_computation.2 | async-start | bytes 2097152 | tf_op jit(solution)/shard_map/all_to_all | solution.py:39
  231.9 110.0 %all-gather.6.cloned.1.call-done = bf16[1024,4096]{0,1:T(8,128)(2,1)} async-done(((bf16[128,4096]{0,1:T(8,128)(2,1)}), bf16[1024,4096]{0,1:T(8,128)(2,1)}) %all-gather.6.cloned.1.call-update) | async-done | bytes 8388624 | tf_op jit(solution)/shard_map/all_gather | solution.py:18
  341.8 11.8 %fusion.19 = f32[32,128,1024]{2,1,0:T(8,128)} fusion(bf16[1024,32,128]{0,2,1:T(8,128)(2,1)} %bitcast.60, bf16[128,4096]{1,0:T(8,128)(2,1)} %param.11), kind=kOutput, calls=%fused_computation.21 | convolution fusion | flops 1073741824 | bytes 26214400 | tf_op jit(solution)/shard_map/qhd,khd->hqk/dot_general | solution.py:56
  353.6 18.0 %convert_reduce_fusion = (f32[32,128]{1,0:T(8,128)S(1)}, bf16[32,128,1024]{2,1,0:T(8,128)(2,1)}) fusion(f32[32,128,1024]{2,1,0:T(8,128)} %fusion.19, pred[1024]{0:T(1024)(128)(4,1)S(1)} %broadcast_bitcast_fusion), kind=kOutput, calls=%fused_computation.1 | output fusion | flops 37749760 | bytes 25183232 | tf_op jit(solution)/shard_map/sub | solution.py:61
  371.6 0.0 all-to-all-done
  371.6 1.5 convolution_convert_fusion.1
  373.0 1.2 copy.21
  374.2 6.9 %fusion.5 = bf16[128,32,128]{0,2,1:T(8,128)(2,1)S(1)} fusion(bf16[32,128,1024]{2,1,0:T(8,128)(2,1)} %get-tuple-element.7, bf16[128,32,128]{2,1,0:T(8,128)(2,1)} %bitcast.63, f32[128,32]{0,1:T(8,128)S(1)} %bitcast.69, pred[128,1024]{1,0:T(32,128)(4,1)S(1)} %fusion.23), kind=kOutput, calls=%fused_computation.12 | convolution fusion | flops 1209532416 | bytes 10633216 | tf_op jit(solution)/shard_map/hqp,phd->qhd/dot_general | solution.py:67
  381.1 1.3 copy.17
  (5 shorter events, 0.0 us)
Async XLA Ops:
  7.2 118.7 %copy-start = (bf16[1,224,4096]{2,1,0:T(8,128)(2,1)S(1)}, bf16[1,224,4096]{2,1,0:T(8,128)(2,1)}, u32[]{:S(2)}) copy-start(bf16[1,224,4096]{2,1,0:T(8,128)(2,1)} %param.15) | copy-start | bytes 5505028
  7.2 62.5 %reduce-scatter.3.cloned.1.call-start = ((), (), s32[]{:S(2)}) async-start(), calls=%async_computation.3 | async-start | bytes 1179648 | tf_op jit(solution)/shard_map/reduce_scatter | solution.py:29
  32.4 89.2 %all-gather.4.cloned.1.call-start = ((), (), s32[]{:S(2)}) async-start(), calls=%async_computation.4 | async-start | bytes 4325376 | tf_op jit(solution)/shard_map/all_gather | solution.py:30
  69.7 153.1 %reduce-scatter.5.cloned.1.call-start = ((), (), s32[]{:S(2)}) async-start(), calls=%async_computation.5 | async-start | bytes 4325376 | tf_op jit(solution)/shard_map/reduce_scatter | solution.py:35
  133.3 1.2 copy-start.1
  133.3 2.5 copy-start.2
  133.3 208.5 %all-gather.6.cloned.1.call-start = ((), (), s32[]{:S(2)}) async-start(), calls=%async_computation.6 | async-start | bytes 9437184 | tf_op jit(solution)/shard_map/all_gather | solution.py:18
  224.8 146.7 %all-to-all-start = ((bf16[8,16,4096]{2,1,0:T(8,128)(2,1)}), bf16[8,16,4096]{2,1,0:T(8,128)(2,1)S(1)}, u32[]{:S(2)}, u32[]{:S(2)}) async-start(bf16[8,16,4096]{2,1,0:T(8,128)(2,1)} %stack.2), calls=%async_computation.2 | async-start | bytes 2097152 | tf_op jit(solution)/shard_map/all_to_all | solution.py:39
Sparse Core Ops, SparseCore 0:
  32.6 37.1 reduce-scatter.2
  72.3 49.3 all-gather.3
  133.4 89.3 reduce-scatter.4
  225.0 116.7 all-gather.5
